TPU v7x, 32 devices: a whole 2x2x4 slice. The times are simulated.
32 devices in a mesh: node: 32 (over z, y, x, core).
Axes of the slice: x: 2, y: 2, z: 4, core: 2. Of those that a mesh axis runs over, the one named last changes fastest.
Arguments:
- event_node: int32 [16384], P('node'), may hold values from 0 to 8191, as said below
- neighbours: int32 [16384, 10], P('node'), may hold values from 0 to 8191, as said below
- event_bucket: int32 [16384], P('node'), may hold values from 0 to 127
- neighbour_bucket: int32 [16384, 10], P('node'), may hold values from 0 to 127
- edge_features: bfloat16 [16384, 128], P('node'), may hold values from -6 to 6
- affinity: float32 [16384, 10], P('node'), may hold values from -320 to 320
- upstream: bfloat16 [16384, 512], P('node'), may hold values from -6 to 6
- node_memory: bfloat16 [8192, 512], P('node'), may hold values from -4 to 4
- edge_weight: bfloat16 [128, 512], replicated, may hold values from -0.5 to 0.5
- time_message: float32 [128, 512], replicated, may hold values from -6 to 6
- input_weight: bfloat16 [512, 1536], replicated, may hold values from -0.25 to 0.25
- hidden_weight: bfloat16 [512, 1536], replicated, may hold values from -0.25 to 0.25
- gate_bias: float32 [1536], replicated, may hold values from -6 to 6
- time_key: float32 [128, 512], replicated, may hold values from -6 to 6
- query_weight: bfloat16 [512, 512], replicated, may hold values from -0.25 to 0.25
- key_weight: bfloat16 [512, 512], replicated, may hold values from -0.25 to 0.25
- value_weight: bfloat16 [512, 512], replicated, may hold values from -0.25 to 0.25
- out_weight: bfloat16 [512, 512], replicated, may hold values from -0.25 to 0.25
Outputs:
- embedding: bfloat16 [16384, 512], P('node')
- new_memory: bfloat16 [8192, 512], P('node')
- grad_query: float32 [512, 512], replicated
- grad_key: float32 [512, 512], replicated
- grad_value: float32 [512, 512], replicated
- grad_out: float32 [512, 512], replicated
Inputs may be any that keep to these rules, and one draw needn't show every extreme that they name: `event_node`: node i belongs to index i // 256 of node. Of the 512 rows of one device, at most 48 name nodes of one index; in every draw one index receives exactly 48 of them from every device. `neighbours`: node i belongs to index i // 256 of node. Of the 5120 entries of one device's rows, at most 320 name nodes of one index, and these name at most 64 distinct nodes; in every draw one index receives exactly 320 entries naming exactly 64 distinct nodes from every device.
All inputs are finite; a program needn't handle non-finite values.
Results may differ from a plain program's by a relative error of at most 0.012.
Values may be sent and summed in bfloat16 or wider, within the bound.
A program may use at most 192 MiB of HBM per device.

v0:
```python
import math

import jax
import jax.numpy as jnp
from jax import lax
from jax.sharding import PartitionSpec as P

HEADS = 2


def table_rows(table, buckets):
    picks = (buckets[:, None] == jnp.arange(table.shape[0], dtype=jnp.int32)[None, :]).astype(
        jnp.float32
    )
    return jnp.dot(
        picks, table, precision=lax.Precision.HIGHEST, preferred_element_type=jnp.float32
    )


def make_message(edge_rows, buckets, edge_weight, time_message):
    before = jnp.dot(edge_rows, edge_weight, preferred_element_type=jnp.float32) + table_rows(
        time_message, buckets
    )
    return jax.nn.silu(before).astype(jnp.bfloat16)


def place_slots(node_ids, node_rows, devices, capacity):
    amount = node_ids.shape[0]
    owners = node_ids // node_rows
    marked = (owners[:, None] == jnp.arange(devices, dtype=jnp.int32)[None, :]).astype(jnp.int32)
    earlier_marks = jnp.cumsum(marked, axis=0) - marked
    ranking = jnp.sum(earlier_marks * marked, axis=1)
    slot_of = owners * capacity + ranking
    holder = (
        jnp.full((devices * capacity,), amount, jnp.int32)
        .at[slot_of]
        .set(jnp.arange(amount, dtype=jnp.int32))
    )
    return (slot_of, holder)


def gru_rows(aggregate, previous, input_weight, hidden_weight, gate_bias):
    columns = previous.shape[1]
    inputs = jnp.dot(aggregate, input_weight, preferred_element_type=jnp.float32) + gate_bias
    hidden = jnp.dot(previous, hidden_weight, preferred_element_type=jnp.float32)
    update = jax.nn.sigmoid(inputs[:, :columns] + hidden[:, :columns])
    resets = jax.nn.sigmoid(inputs[:, columns : 2 * columns] + hidden[:, columns : 2 * columns])
    candidate = jnp.tanh(inputs[:, 2 * columns :] + resets * hidden[:, 2 * columns :])
    return (1.0 - update) * candidate + update * previous.astype(jnp.float32)


def attend(
    target,
    neighbour_rows,
    neighbour_bucket,
    affinity,
    time_key,
    query_weight,
    key_weight,
    value_weight,
    out_weight,
):
    events, fanout, columns = neighbour_rows.shape
    head_size = columns // HEADS
    query = (
        jnp.dot(target, query_weight, preferred_element_type=jnp.float32)
        .astype(jnp.bfloat16)
        .reshape(events, HEADS, head_size)
    )
    flat_rows = neighbour_rows.reshape(events * fanout, columns)
    key_rows = jnp.dot(flat_rows, key_weight, preferred_element_type=jnp.float32) + table_rows(
        time_key, neighbour_bucket.reshape(-1)
    )
    key_rows = key_rows.astype(jnp.bfloat16).reshape(events, fanout, HEADS, head_size)
    value_rows = (
        jnp.dot(flat_rows, value_weight, preferred_element_type=jnp.float32)
        .astype(jnp.bfloat16)
        .reshape(events, fanout, HEADS, head_size)
    )
    scores = jnp.einsum(
        "ehd,enhd->ehn", query, key_rows, preferred_element_type=jnp.float32
    ) / math.sqrt(head_size)
    scores = scores + affinity[:, None, :]
    probs = jax.nn.softmax(scores, axis=-1).astype(jnp.bfloat16)
    mixed = jnp.einsum("ehn,enhd->ehd", probs, value_rows, preferred_element_type=jnp.float32)
    mixed = mixed.astype(jnp.bfloat16).reshape(events, columns)
    return (
        jnp.dot(mixed, out_weight, preferred_element_type=jnp.float32) + target.astype(jnp.float32)
    ).astype(jnp.bfloat16)


def shards(
    event_node,
    neighbours,
    event_bucket,
    neighbour_bucket,
    edge_features,
    affinity,
    upstream,
    node_memory,
    edge_weight,
    time_message,
    input_weight,
    hidden_weight,
    gate_bias,
    time_key,
    query_weight,
    key_weight,
    value_weight,
    out_weight,
):
    devices = lax.axis_size("node")
    node_rows = node_memory.shape[0]
    columns = node_memory.shape[1]
    events = neighbours.shape[0]
    fanout = neighbours.shape[1]
    cap_message = 3 * events // devices
    slot_event, holder_event = place_slots(event_node, node_rows, devices, cap_message)
    filled = holder_event < events
    source = jnp.minimum(holder_event, events - 1)
    local_target = jnp.where(filled, event_node[source] % node_rows, node_rows).reshape(
        devices, cap_message
    )
    messages = make_message(edge_features, event_bucket, edge_weight, time_message)
    outgoing = jnp.where(filled[:, None], messages[source], jnp.zeros((), jnp.bfloat16)).reshape(
        devices, cap_message, -1
    )
    rows_in, arrived = (
        lax.all_to_all(local_target, "node", split_axis=0, concat_axis=0, tiled=True),
        lax.all_to_all(outgoing, "node", split_axis=0, concat_axis=0, tiled=True),
    )
    arrived = arrived.reshape(devices * cap_message, -1)
    flat_in = rows_in.reshape(-1)
    totals = jax.ops.segment_sum(arrived.astype(jnp.float32), flat_in, num_segments=node_rows + 1)[
        :node_rows
    ]
    counts = jax.ops.segment_sum(
        jnp.ones(flat_in.shape, jnp.float32), flat_in, num_segments=node_rows + 1
    )[:node_rows]
    aggregate = (totals / jnp.maximum(counts, 1.0)[:, None]).astype(jnp.bfloat16)
    updated = gru_rows(aggregate, node_memory, input_weight, hidden_weight, gate_bias)
    new_memory = jnp.where(counts[:, None] > 0, updated, node_memory.astype(jnp.float32)).astype(
        jnp.bfloat16
    )
    padded = jnp.concatenate([new_memory, jnp.zeros((1, columns), jnp.bfloat16)], axis=0)
    returned = lax.all_to_all(
        padded[flat_in].reshape(devices, cap_message, columns),
        "node",
        split_axis=0,
        concat_axis=0,
        tiled=True,
    )
    target = returned.reshape(-1, columns)[slot_event]
    entries = neighbours.reshape(-1)
    whole_table = lax.all_gather(new_memory, "node", axis=0, tiled=True)
    nearby = whole_table[entries].reshape(events, fanout, columns)

    def forward(weight_q, weight_k, weight_v, weight_o):
        return attend(
            target,
            nearby,
            neighbour_bucket,
            affinity,
            time_key,
            weight_q,
            weight_k,
            weight_v,
            weight_o,
        )

    embedding, pullback = jax.vjp(forward, query_weight, key_weight, value_weight, out_weight)
    grad_q, grad_k, grad_v, grad_o = pullback(upstream)
    summed = lax.psum(
        (
            grad_q.astype(jnp.float32),
            grad_k.astype(jnp.float32),
            grad_v.astype(jnp.float32),
            grad_o.astype(jnp.float32),
        ),
        "node",
    )
    factor = 1.0 / math.sqrt(events * devices)
    return (
        embedding,
        new_memory,
        summed[0] * factor,
        summed[1] * factor,
        summed[2] * factor,
        summed[3] * factor,
    )


def solution(mesh):
    placed = (
        P("node"),
        P("node", None),
        P("node"),
        P("node", None),
        P("node", None),
        P("node", None),
        P("node", None),
        P("node", None),
        P(),
        P(),
        P(),
        P(),
        P(),
        P(),
        P(),
        P(),
        P(),
        P(),
    )
    return jax.shard_map(
        shards,
        mesh=mesh,
        in_specs=placed,
        out_specs=(P("node", None), P("node", None), P(), P(), P(), P()),
        check_vma=False,
    )
```

profile of v0, /device:TPU:0, one launch (start us, length us, event | category | flops | bytes accessed | tf_op | source)
XLA Modules:
  0.0 490.4 jit_solution(15523726660007874801)
XLA Ops:
  7.2 0.8 add_select_fusion.1
  8.7 1.2 reduce-window.6
  11.0 2.5 scatter_custom_fusion
  13.5 9.5 %gather_fusion = s32[1536]{0:T(1024)S(1)} fusion(s32[512]{0:T(512)S(1)} %copy-done.2, s32[2048]{0:T(1024)S(1)} %pad_clamp_fusion.1), kind=kCustom, calls=%fused_computation | custom fusion | bytes 18432 | tf_op jit(solution)/shard_map/gather | solution.py:121
  23.7 7.3 %all-to-all-start = ((s32[32,1,48]{2,1,0:T(1,128)}), s32[32,1,48]{2,1,0:T(1,128)S(1)}, u32[]{:S(2)}, u32[]{:S(2)}) async-start(s32[32,1,48]{2,1,0:T(1,128)} %all_to_all.12), calls=%async_computation | async-start | bytes 32768 | tf_op jit(solution)/shard_map/all_to_all | solution.py:129
  32.1 5.4 %gather_fusion.1 = bf16[1536,512]{1,0:T(8,128)(2,1)} fusion(bf16[512,512]{1,0:T(8,128)(2,1)S(1)} %multiply_convert_fusion.2, s32[2048]{0:T(1024)S(1)} %pad_clamp_fusion.1), kind=kCustom, calls=%fused_computation.1 | custom fusion | bytes 3151872 | tf_op jit(solution)/shard_map/gather | solution.py:125
  37.7 2.9 broadcast_select_fusion
  40.5 5.8 %all-to-all-start.1 = ((bf16[32,48,512]{2,1,0:T(8,128)(2,1)}), bf16[32,48,512]{2,1,0:T(8,128)(2,1)S(1)}, u32[]{:S(2)}, u32[]{:S(2)}) async-start(bf16[32,48,512]{2,1,0:T(8,128)(2,1)} %broadcast_select_fusion), calls=%async_computation.1 | async-start | bytes 3145728 | tf_op jit(solution)/shard_map/all_to_all | solution.py:130
  46.4 1.7 fusion.57
  49.4 11.1 %scatter_custom_fusion.1 = f32[257]{0:T(512)S(1)} fusion(s32[1536]{0:T(1024)S(1)} %reshape.218, f32[1536]{0:T(1024)S(1)} %broadcast.111, f32[]{:T(128)} %constant.22.clone.1), kind=kCustom, calls=%fused_computation.117 | custom fusion | flops 1536 | bytes 1032 | tf_op jit(solution)/shard_map/scatter-add | solution.py:137
  60.6 23.4 %all-to-all-done.1 = bf16[32,48,512]{2,1,0:T(8,128)(2,1)S(1)} async-done(((bf16[32,48,512]{2,1,0:T(8,128)(2,1)}), bf16[32,48,512]{2,1,0:T(8,128)(2,1)S(1)}, u32[]{:S(2)}, u32[]{:S(2)}) %all-to-all-start.1) | async-done | bytes 1572896 | tf_op jit(solution)/shard_map/all_to_all | solution.py:130
  84.0 11.2 %scatter_custom_fusion.2 = f32[257,512]{1,0:T(8,128)} fusion(s32[1536]{0:T(1024)S(1)} %reshape.218, bf16[1536,512]{1,0:T(8,128)(2,1)S(1)} %bitcast.92, f32[]{:T(128)} %constant.22.clone.1), kind=kCustom, calls=%fused_computation.30 | custom fusion | flops 1572864 | bytes 2099204 | tf_op jit(solution)/shard_map/scatter-add | solution.py:134
  95.3 2.2 convolution_add_fusion
  97.5 1.1 fusion.22
  98.7 1.0 concatenate.3
  99.7 5.4 %gather_fusion.2 = bf16[1536,512]{1,0:T(8,128)(2,1)} fusion(bf16[257,512]{1,0:T(8,128)(2,1)S(1)} %concatenate.3, s32[2048]{0:T(1024)S(1)} %pad_clamp_fusion), kind=kCustom, calls=%fused_computation.2 | custom fusion | bytes 3151872 | tf_op jit(solution)/shard_map/gather | solution.py:147
  105.2 3.8 all-to-all-start.2
  111.0 50.4 %all-to-all-done.2 = bf16[32,48,512]{2,1,0:T(8,128)(2,1)S(1)} async-done(((bf16[32,48,512]{2,1,0:T(8,128)(2,1)}), bf16[32,48,512]{2,1,0:T(8,128)(2,1)S(1)}, u32[]{:S(2)}, u32[]{:S(2)}) %all-to-all-start.2) | async-done | bytes 1572896 | tf_op jit(solution)/shard_map/all_to_all | solution.py:146
  161.5 2.0 gather_fusion.3
  163.4 1.5 convolution_convert_fusion.6
  165.4 24.3 %all-gather.2.cloned.1.call-done = bf16[8192,512]{1,0:T(8,128)(2,1)} async-done(((bf16[256,512]{1,0:T(8,128)(2,1)}), bf16[8192,512]{1,0:T(8,128)(2,1)}) %all-gather.2.cloned.1.call-update) | async-done | bytes 8388624 | tf_op jit(solution)/shard_map/all_gather | solution.py:155
  189.7 26.0 %gather_fusion.4 = bf16[5120,512]{1,0:T(8,128)(2,1)} fusion(bf16[8192,512]{1,0:T(8,128)(2,1)} %all-gather.2.cloned.1.call-done, s32[5120]{0:T(1024)S(1)} %broadcast_clamp_fusion), kind=kCustom, calls=%fused_computation.4 | custom fusion | bytes 10506240 | tf_op jit(solution)/shard_map/gather | solution.py:156
  215.8 4.8 fusion.58
  220.6 6.8 %add_convert_fusion = bf16[5120,512]{1,0:T(8,128)(2,1)} fusion(f32[5120,512]{1,0:T(8,128)S(1)} %fusion.58, f32[128,512]{1,0:T(8,128)S(1)} %copy-done.17, s32[5120]{0:T(1024)S(1)} %eq.63), kind=kOutput, calls=%fused_computation.13 | convolution fusion | flops 4032430080 | bytes 16011264 | tf_op jit(solution)/shard_map/jvp()/dot_general | solution.py:15
  227.4 8.3 %reshape.160 = bf16[512,10,2,256]{3,2,1,0:T(2,128)(2,1)} reshape(bf16[5120,512]{1,0:T(8,128)(2,1)} %add_convert_fusion) | data formatting | bytes 10485760 | tf_op jit(solution)/shard_map/jvp()/reshape | solution.py:74
  235.7 9.7 %multiply_reduce_fusion.1 = f32[512,2,10]{1,2,0:T(8,128)S(1)} fusion(f32[512,2,256]{2,1,0:T(2,128)S(1)} %copy.50, bf16[512,10,2,256]{3,2,1,0:T(2,128)(2,1)} %reshape.160), kind=kLoop, calls=%fused_computation.10 | loop fusion | flops 7854080 | bytes 6332416 | tf_op jit(solution)/shard_map/jvp(ehd,enhd->ehn)/dot_general | solution.py:80
  245.5 4.8 fusion.56
  250.4 4.6 convolution_convert_fusion
  254.9 8.3 %reshape.161 = bf16[512,10,2,256]{3,2,1,0:T(2,128)(2,1)} reshape(bf16[5120,512]{1,0:T(8,128)(2,1)} %convolution_convert_fusion) | data formatting | bytes 10485760 | tf_op jit(solution)/shard_map/jvp()/reshape | solution.py:78
  263.3 9.9 %multiply_reduce_fusion = bf16[512,2,10]{1,2,0:T(8,128)(2,1)S(1)} fusion(f32[512,2,256]{2,1,0:T(2,128)S(1)} %copy.51, bf16[512,10,2,256]{3,2,1,0:T(2,128)(2,1)} %reshape.161), kind=kLoop, calls=%fused_computation.9 | loop fusion | flops 7854080 | bytes 6311936 | tf_op jit(solution)/shard_map/transpose(jvp(ehn,enhd->ehd))/dot_general | solution.py:85
  273.2 1.5 fusion.9
  274.8 4.7 fusion.54
  279.5 8.1 %copy.39 = bf16[512,2,10,1]{2,3,1,0:T(2,128)(2,1)S(1)} copy(bf16[512,2,10,1]{1,2,0,3:T(8,128)(2,1)} %get-tuple-element.14) | data formatting | bytes 40960 | tf_op jit(solution)/shard_map/jvp()/convert_element_type | solution.py:84
  287.6 4.0 fusion.3
  292.2 9.1 %multiply_convert_fusion.1 = bf16[512,2,10,256]{3,1,2,0:T(2,128)(2,1)} fusion(f32[512,2,256]{2,1,0:T(2,128)S(1)} %copy.50, f32[512,2,10]{1,2,0:T(8,128)S(1)} %copy-done.3), kind=kLoop, calls=%fused_computation.12 | loop fusion | flops 5242880 | bytes 6332416 | tf_op jit(solution)/shard_map/transpose(jvp(ehd,enhd->ehn))/convert_element_type | solution.py:80
  301.4 8.4 %copy.47 = bf16[512,2,10,1]{2,3,1,0:T(2,128)(2,1)S(1)} copy(f32[512,2,10,1]{1,2,0,3:T(8,128)} %bitcast.82) | data formatting | bytes 61440 | tf_op jit(solution)/shard_map/transpose(jvp())/div | solution.py:80
  309.8 4.0 fusion.1
  314.5 1.4 fusion.18
  315.9 0.9 copy.57
  317.6 3.9 fusion.17
  321.4 8.4 %multiply_convert_fusion = bf16[512,2,256,10]{2,1,3,0:T(2,128)(2,1)S(1)} fusion(f32[512,2,256]{2,1,0:T(2,128)S(1)} %copy-done.7, f32[512,2,10]{1,2,0:T(8,128)S(1)} %copy-done.4), kind=kLoop, calls=%fused_computation.11 | loop fusion | flops 5242880 | bytes 6332416 | tf_op jit(solution)/shard_map/transpose(jvp(ehn,enhd->ehd))/convert_element_type | solution.py:85
  329.9 0.9 copy.58
  330.8 3.9 fusion.16
  334.6 1.4 fusion.19
  336.1 1.2 fusion.20
  337.3 141.0 %all-reduce.4.cloned.1.call-done = (f32[512,512]{1,0:T(8,128)}, f32[512,512]{1,0:T(8,128)}, f32[512,512]{1,0:T(8,128)}, f32[512,512]{1,0:T(8,128)}) async-done(((f32[512,512]{1,0:T(8,128)}, f32[512,512]{1,0:T(8,128)}, f32[512,512]{1,0:T(8,128)}, f32[512,512]{1,0:T(8,128)}), (f32[512,512]{1,0:T(8,128)}, f32[512,512]{1,0:T(8,128)}, f32[512,512]{1,0:T(8,128)}, ...) | async-done | bytes 4194320 | tf_op jit(solution)/shard_map/psum | solution.py:173
  478.3 3.2 broadcast_multiply_fusion.2
  481.5 1.5 broadcast_multiply_fusion
  (115 shorter events, 9.7 us)
Async XLA Ops:
  7.2 39.3 %copy-start = (bf16[512,1536]{1,0:T(8,128)(2,1)S(1)}, bf16[512,1536]{1,0:T(8,128)(2,1)}, u32[]{:S(2)}) copy-start(bf16[512,1536]{1,0:T(8,128)(2,1)} %param.29) | copy-start | bytes 4718596
  7.2 6.3 %copy-start.2 = (s32[512]{0:T(512)S(1)}, s32[512]{0:T(512)}, u32[]{:S(2)}) copy-start(s32[512]{0:T(512)} %param.18) | copy-start | bytes 6148
  13.4 17.6 %copy-start.18 = (f32[128,512]{1,0:T(8,128)S(1)}, f32[128,512]{1,0:T(8,128)}, u32[]{:S(2)}) copy-start(f32[128,512]{1,0:T(8,128)} %param.27) | copy-start | bytes 786436
  13.5 17.6 %copy-start.22 = (s32[512]{0:T(512)S(1)}, s32[512]{0:T(512)}, u32[]{:S(2)}) copy-start(s32[512]{0:T(512)} %param.20) | copy-start | bytes 6148
  13.5 18.2 %copy-start.24 = (bf16[512,128]{1,0:T(8,128)(2,1)S(1)}, bf16[512,128]{1,0:T(8,128)(2,1)}, u32[]{:S(2)}) copy-start(bf16[512,128]{1,0:T(8,128)(2,1)} %param.22) | copy-start | bytes 393220
  13.5 18.2 %copy-start.25 = (bf16[128,512]{1,0:T(8,128)(2,1)S(1)}, bf16[128,512]{1,0:T(8,128)(2,1)}, u32[]{:S(2)}) copy-start(bf16[128,512]{1,0:T(8,128)(2,1)} %param.26) | copy-start | bytes 393220
  23.7 16.8 %all-to-all-start = ((s32[32,1,48]{2,1,0:T(1,128)}), s32[32,1,48]{2,1,0:T(1,128)S(1)}, u32[]{:S(2)}, u32[]{:S(2)}) async-start(s32[32,1,48]{2,1,0:T(1,128)} %all_to_all.12), calls=%async_computation | async-start | bytes 32768 | tf_op jit(solution)/shard_map/all_to_all | solution.py:129
  37.6 8.8 %copy-start.15 = (bf16[256,512]{1,0:T(8,128)(2,1)S(1)}, bf16[256,512]{1,0:T(8,128)(2,1)}, u32[]{:S(2)}) copy-start(bf16[256,512]{1,0:T(8,128)(2,1)} %param.25) | copy-start | bytes 786436
  40.5 54.7 %copy-start.26 = (f32[1536]{0:T(1024)S(1)}, f32[1536]{0:T(1024)}, u32[]{:S(2)}) copy-start(f32[1536]{0:T(1024)} %param.30) | copy-start | bytes 18436
  40.5 43.5 %all-to-all-start.1 = ((bf16[32,48,512]{2,1,0:T(8,128)(2,1)}), bf16[32,48,512]{2,1,0:T(8,128)(2,1)S(1)}, u32[]{:S(2)}, u32[]{:S(2)}) async-start(bf16[32,48,512]{2,1,0:T(8,128)(2,1)} %broadcast_select_fusion), calls=%async_computation.1 | async-start | bytes 3145728 | tf_op jit(solution)/shard_map/all_to_all | solution.py:130
  46.4 143.4 %all-gather.2.cloned.1.call-start = ((), (), s32[]{:S(2)}) async-start(), calls=%async_computation.3 | async-start | bytes 8650752 | tf_op jit(solution)/shard_map/all_gather | solution.py:155
  48.2 49.3 %copy-start.8 = (f32[256,1536]{1,0:T(8,128)S(1)}, f32[256,1536]{1,0:T(8,128)}, u32[]{:S(2)}) copy-start(f32[256,1536]{1,0:T(8,128)} %fusion.57) | copy-start | bytes 4718596
  99.7 9.3 %copy-start.19 = (s32[512,10]{0,1:T(8,128)S(1)}, s32[512,10]{0,1:T(8,128)}, u32[]{:S(2)}) copy-start(s32[512,10]{0,1:T(8,128)} %param.19) | copy-start | bytes 61444
  99.7 9.6 %copy-start.20 = (s32[512,10]{0,1:T(8,128)S(1)}, s32[512,10]{0,1:T(8,128)}, u32[]{:S(2)}) copy-start(s32[512,10]{0,1:T(8,128)} %param.21) | copy-start | bytes 61444
  105.2 4.5 copy-start.21
  105.2 4.7 copy-start.9
  105.2 4.7 copy-start.11
  105.2 56.3 %all-to-all-start.2 = ((bf16[32,48,512]{2,1,0:T(8,128)(2,1)}), bf16[32,48,512]{2,1,0:T(8,128)(2,1)S(1)}, u32[]{:S(2)}, u32[]{:S(2)}) async-start(bf16[32,48,512]{2,1,0:T(8,128)(2,1)} %bitcast.6), calls=%async_computation.2 | async-start | bytes 3145728 | tf_op jit(solution)/shard_map/all_to_all | solution.py:146
  108.9 369.4 %all-reduce.4.cloned.1.call-start = ((), (), s32[]{:S(2)}) async-start(), calls=%async_computation.4 | async-start | bytes 8388608 | tf_op jit(solution)/shard_map/psum | solution.py:173
  110.9 152.3 %copy-start.6 = (f32[512,2,256]{2,1,0:T(2,128)}, f32[512,2,256]{2,1,0:T(2,128)S(1)}, u32[]{:S(2)}) copy-start(f32[512,2,256]{2,1,0:T(2,128)S(1)} %copy.51) | copy-start | bytes 3145732
  165.4 50.4 %copy-start.16 = (bf16[512,512]{1,0:T(8,128)(2,1)S(1)}, bf16[512,512]{1,0:T(8,128)(2,1)}, u32[]{:S(2)}) copy-start(bf16[512,512]{1,0:T(8,128)(2,1)} %param.33) | copy-start | bytes 1572868
  215.8 4.9 copy-start.17
  235.7 14.6 %slice-start = ((s8[5242880]{0:T(1024)(128)(4,1)}), s8[4194304]{0:T(1024)(128)(4,1)S(1)}, s32[]{:S(2)}) async-start(s8[5242880]{0:T(1024)(128)(4,1)} %bitcast.83), calls=%async_computation.5 | async-start | bytes 8388608
  245.5 4.9 slice-start.1
  245.5 4.9 copy-start.23
  263.3 9.9 %copy-start.5 = (f32[512,2,10]{1,2,0:T(8,128)S(1)}, f32[512,2,10]{1,2,0:T(8,128)}, u32[]{:S(2)}) copy-start(f32[512,2,10]{1,2,0:T(8,128)} %get-tuple-element.16) | copy-start | bytes 122884
  287.6 4.7 copy-start.3
  301.4 14.5 %slice-start.4 = ((s8[5242880]{0:T(1024)(128)(4,1)}), s8[1048576]{0:T(1024)(128)(4,1)S(1)}, s32[]{:S(2)}) async-start(s8[5242880]{0:T(1024)(128)(4,1)} %bitcast.88), calls=%async_computation.9 | async-start | bytes 2097152
  309.8 6.1 %slice-start.5 = ((s8[5242880]{0:T(1024)(128)(4,1)}), s8[4194304]{0:T(1024)(128)(4,1)S(1)}, s32[]{:S(2)}) async-start(s8[5242880]{0:T(1024)(128)(4,1)} %bitcast.88), calls=%async_computation.10 | async-start | bytes 8388608
  314.5 2.6 slice-start.2
  315.9 1.6 slice-start.3
  317.6 3.9 copy-start.4
  317.6 3.9 copy-start.7
  330.7 3.9 copy-start.10
  334.6 1.5 copy-start.12
  478.3 3.3 copy-start.13
  478.3 3.3 copy-start.14
  478.3 4.8 copy-start.1
Sparse Core Ops, SparseCore 0:
  98.7 90.9 all-gather.1
  336.2 142.0 all-reduce.3
where the time goes:
time: 499 us; the launch traced here: 490 us
  waiting for transfers between devices  239 us (48%)
  local copies, waits for them, and re-layouts  92.4 us (19%)
  other arithmetic  83.7 us (17%)
  matrix products  43 us (9%)
  starting transfers between devices  17 us (3%)
  between operations  15.1 us (3%)
    psum x1, waiting for transfers between devices, shards(): lax.psum((grad_q.astype(jnp.float32), grad_k.astype(jnp.float32), grad_v....  141 us
    all_to_all x1, waiting for transfers between devices, shards(): lax.all_to_all(padded[flat_in].reshape(devices, cap_message, columns), 'n...  50.4 us
    gather x1, local copies, waits for them, and re-layouts, shards(): nearby = whole_table[entries].reshape(events, fanout, columns)  26 us
    all_gather x1, waiting for transfers between devices, shards(): whole_table = lax.all_gather(new_memory, 'node', axis=0, tiled=True)  24.3 us
    all_to_all x1, waiting for transfers between devices, shards(): lax.all_to_all(outgoing, 'node', split_axis=0, concat_axis=0, tiled=True)  23.4 us
    scatter-add x1, other arithmetic, shards(): jax.ops.segment_sum(arrived.astype(jnp.float32), flat_in, num_segments=no...  11.2 us
    scatter-add x1, other arithmetic, shards(): jax.ops.segment_sum(jnp.ones(flat_in.shape, jnp.float32), flat_in, num_se...  11.1 us
  transfers between devices with their start and end apart: 5, of which 4 were waited for; matrix products, arithmetic and copies ran while one was open for 8% of the time, Pallas kernels for 0%

commit v1 on v0

v1 whole, which is shorter than its diff:
```python
import functools
import math

import jax
import jax.numpy as jnp
from jax import lax
from jax.experimental import pallas as pl
from jax.experimental.pallas import tpu as pltpu
from jax.sharding import PartitionSpec as P

HEADS = 2
LANES = 128
GROUP = 32
BF = jnp.bfloat16
F32 = jnp.float32
VMEM_LIMIT = 60 * 1024 * 1024
RESIDENT_LIMIT = 20 * 1024 * 1024
NT = (((1,), (1,)), ((), ()))
TN = (((0,), (0,)), ((), ()))


def mm(a, b):
    return jnp.dot(a, b, preferred_element_type=F32)


def mm_nt(a, b):
    return lax.dot_general(a, b, NT, preferred_element_type=F32)


def mm_tn(a, b):
    return lax.dot_general(a, b, TN, preferred_element_type=F32)


def halves(table):
    high = table.astype(BF)
    low = (table - high.astype(F32)).astype(BF)
    return high, low


def memory_kernel(
    devices,
    events,
    slots,
    chunk,
    feats,
    meta,
    owners,
    memory,
    edge_weight,
    time_message,
    input_weight,
    hidden_weight,
    gate_bias,
    out_memory,
    out_table,
    sel,
    picked,
    picked_meta,
    totals,
    counts,
    wide,
):
    me = lax.axis_index("node")
    rows = memory.shape[0]
    columns = memory.shape[1]
    stride = columns // LANES
    mine = owners[...] == me.astype(F32)
    before = lax.broadcasted_iota(jnp.int32, (events, events), 0) < lax.broadcasted_iota(
        jnp.int32, (events, events), 1
    )
    rank = mm(mine.astype(F32).astype(BF), before.astype(F32).astype(BF))
    sel[...] = jnp.where(mine, rank, -1.0)
    slot_ids = lax.broadcasted_iota(jnp.int32, (slots, events), 0).astype(F32)

    def pick(step, carry):
        for half in range(4):
            source = step * 4 + half
            hits = (slot_ids == sel[pl.ds(source, 1), :]).astype(F32).astype(BF)
            at = pl.ds(pl.multiple_of(source * slots, slots), slots)
            picked[at, :] = mm(hits, feats[source, :events, :]).astype(BF)
            picked_meta[at, :] = mm_nt(hits, meta[source])
        return carry

    lax.fori_loop(0, devices // 4, pick, 0)
    totals[...] = jnp.zeros_like(totals)
    counts[...] = jnp.zeros_like(counts)
    high, low = halves(time_message[...])
    weight = edge_weight[...]

    def add(step, carry):
        at = pl.ds(pl.multiple_of(step * chunk, chunk), chunk)
        info = picked_meta[at, :]
        node, bucket, valid = info[:, 0:1], info[:, 1:2], info[:, 2:3]
        lanes = lax.broadcasted_iota(jnp.int32, (chunk, high.shape[0]), 1).astype(F32)
        picks = (lanes == bucket).astype(F32).astype(BF)
        pre = mm(picked[at, :], weight) + mm(picks, high) + mm(picks, low)
        message = (pre / (1.0 + jnp.exp(-pre))).astype(BF)
        ids = lax.broadcasted_iota(jnp.int32, (chunk, rows), 1).astype(F32)
        hot = jnp.where(ids == node, valid, 0.0).astype(BF)
        totals[...] += mm_tn(hot, message)
        counts[...] += mm_tn(hot, jnp.ones((chunk, LANES), BF))
        return carry

    lax.fori_loop(0, devices * slots // chunk, add, 0)
    count = counts[:, 0:1]
    aggregate = (totals[...] / jnp.maximum(count, 1.0)).astype(BF)
    previous = memory[...]

    def gate(which):
        cut = slice(which * columns, (which + 1) * columns)
        return (
            mm(aggregate, input_weight[:, cut]) + gate_bias[:, cut],
            mm(previous, hidden_weight[:, cut]),
        )

    from_input, from_hidden = gate(0)
    update = jax.nn.sigmoid(from_input + from_hidden)
    from_input, from_hidden = gate(1)
    resets = jax.nn.sigmoid(from_input + from_hidden)
    from_input, from_hidden = gate(2)
    candidate = jnp.tanh(from_input + resets * from_hidden)
    old = previous.astype(F32)
    fresh = (1.0 - update) * candidate + update * old
    fresh = jnp.where(count > 0, fresh, old)
    out_memory[...] = fresh.astype(BF)
    for part in range(stride):
        wide[pl.ds(part, rows, stride=stride), :] = fresh[:, part * LANES : (part + 1) * LANES]
    out_table[...] = wide[...].astype(BF)


def event_kernel(
    resident,
    events,
    fanout,
    ids,
    source,
    buckets,
    affinity,
    upstream,
    time_key,
    query_weight,
    key_weight,
    value_weight,
    out_weight,
    embedding,
    grads,
    *scratch,
):
    columns = upstream.shape[1]
    head = columns // HEADS
    stride = columns // LANES
    if resident:
        landing, table, near, sems, *scratch = scratch
        parts = sems.shape[0]
        size = landing.shape[0] // parts
        copies = []
        for part in range(parts):
            at = pl.ds(part * size, size)
            copies.append(pltpu.make_async_copy(source.at[at], landing.at[at], sems.at[part]))
            copies[-1].start()
    else:
        near = source
        (*scratch,) = scratch
    target, query, back, pull, mix, hits, tq = scratch
    heads = [slice(h * head, (h + 1) * head) for h in range(HEADS)]
    high, low = halves(time_key[...])

    back[...] = mm_nt(upstream[...], out_weight[...]).astype(BF)
    for h, cut in enumerate(heads):
        pull[HEADS + h] = mm_nt(back[:, cut], value_weight[:, cut])

    if resident:
        step_rows = 256
        for part in range(parts):
            copies[part].wait()

            def widen(step, carry, part=part):
                at = pl.ds(pl.multiple_of(part * size + step * step_rows, step_rows), step_rows)
                table[at, :] = landing[at, :].astype(F32)
                return carry

            lax.fori_loop(0, size // step_rows, widen, 0)

        unroll = 16

        def fetch(step, carry):
            for lane in range(unroll):
                row = step * unroll + lane
                start = pl.multiple_of(ids[row], stride)
                near[pl.ds(pl.multiple_of(row * stride, stride), stride), :] = table[
                    pl.ds(start, stride), :
                ]
            return carry

        lax.fori_loop(0, (fanout + 1) * events // unroll, fetch, 0)

    for part in range(stride):
        target[:, part * LANES : (part + 1) * LANES] = near[
            pl.ds(fanout * events * stride + part, events, stride=stride), :
        ].astype(BF)
    query[...] = mm(target[...], query_weight[...]).astype(BF)
    for h, cut in enumerate(heads):
        pull[h] = mm_nt(query[:, cut], key_weight[:, cut])
        tq[h] = mm_nt(query[:, cut], high[:, cut]) + mm_nt(query[:, cut], low[:, cut])

    size = 32
    scale = 1.0 / math.sqrt(head)
    lane = lax.broadcasted_iota(jnp.int32, (size, LANES), 1)
    masks = [(lane >= h * GROUP) & (lane < h * GROUP + fanout) for h in range(HEADS)]

    def per_head(values, op, fill):
        out = jnp.zeros((size, LANES), F32)
        for mask in masks:
            out = jnp.where(
                mask, op(jnp.where(mask, values, fill), axis=1, keepdims=True), out
            )
        return out

    def block(step, carry):
        first = pl.multiple_of(step * size, size)
        at = pl.ds(first, size)
        names = buckets[at, :]

        def rows_of(j, part):
            return near[pl.ds((j * events + first) * stride + part, size, stride=stride), :]

        raw = jnp.zeros((size, LANES), F32)
        for j in range(fanout):
            same = lane == names[:, j : j + 1]
            nearby = [rows_of(j, part) for part in range(stride)]
            for k in range(2 * HEADS):
                total = nearby[0] * pull[k, at, 0:LANES]
                for part in range(1, stride):
                    total += nearby[part] * pull[k, at, part * LANES : (part + 1) * LANES]
                if k < HEADS:
                    total += jnp.where(same, tq[k, at, :], 0.0)
                raw = jnp.where(
                    lane == k * GROUP + j, jnp.sum(total, axis=1, keepdims=True), raw
                )
        scores = raw * scale + affinity[at, :]
        active = masks[0]
        for mask in masks[1:]:
            active = active | mask
        top = per_head(scores, jnp.max, -3.0e38)
        raised = jnp.where(active, jnp.exp(jnp.where(active, scores - top, 0.0)), 0.0)
        below = per_head(raised, jnp.sum, 0.0)
        probs = jnp.where(active, raised / jnp.where(active, below, 1.0), 0.0)
        turned = pltpu.roll(raw, HEADS * GROUP, axis=1).astype(BF).astype(F32)
        slopes = jnp.where(active, turned, 0.0)
        inner = per_head(probs * slopes, jnp.sum, 0.0)
        slopes = probs * (slopes - inner) * scale
        blend = jnp.where(
            active, probs.astype(BF).astype(F32), pltpu.roll(slopes, HEADS * GROUP, axis=1)
        )
        spread = [
            [
                jnp.broadcast_to(blend[:, k * GROUP + j : k * GROUP + j + 1], (size, LANES))
                for j in range(fanout)
            ]
            for k in range(2 * HEADS)
        ]
        for h in range(HEADS):
            total = jnp.zeros((size, LANES), F32)
            for j in range(fanout):
                total += jnp.where(lane == names[:, j : j + 1], spread[HEADS + h][j], 0.0)
            hits[h, at, :] = total.astype(BF)
        for part in range(stride):
            sums = [jnp.zeros((size, LANES), F32) for _ in range(2 * HEADS)]
            for j in range(fanout):
                nearby = rows_of(j, part)
                for k in range(2 * HEADS):
                    sums[k] += spread[k][j] * nearby
            for k in range(2 * HEADS):
                mix[k, at, part * LANES : (part + 1) * LANES] = sums[k].astype(BF)
        return carry

    lax.fori_loop(0, events // size, block, 0)

    for h, cut in enumerate(heads):
        grads[2 * columns : 3 * columns, cut] = mm_tn(mix[h], back[:, cut]).astype(BF)
        grads[columns : 2 * columns, cut] = mm_tn(mix[HEADS + h], query[:, cut]).astype(BF)
    for h, cut in enumerate(heads):
        back[:, cut] = mm(mix[h], value_weight[:, cut]).astype(BF)
        query[:, cut] = (
            mm(mix[HEADS + h], key_weight[:, cut])
            + mm(hits[h], high[:, cut])
            + mm(hits[h], low[:, cut])
        ).astype(BF)
    grads[:columns, :] = mm_tn(target[...], query[...]).astype(BF)
    grads[3 * columns :, :] = mm_tn(back[...], upstream[...]).astype(BF)
    embedding[...] = (mm(back[...], out_weight[...]) + target[...].astype(F32)).astype(BF)


def shards(
    event_node,
    neighbours,
    event_bucket,
    neighbour_bucket,
    edge_features,
    affinity,
    upstream,
    node_memory,
    edge_weight,
    time_message,
    input_weight,
    hidden_weight,
    gate_bias,
    time_key,
    query_weight,
    key_weight,
    value_weight,
    out_weight,
):
    devices = lax.axis_size("node")
    node_rows, columns = node_memory.shape
    events, fanout = neighbours.shape
    features = edge_features.shape[1]
    stride = columns // LANES
    slots = -(-(3 * events // devices) // 16) * 16
    vmem = pl.BlockSpec(memory_space=pltpu.VMEM)
    smem = pl.BlockSpec(memory_space=pltpu.SMEM)

    info_rows = events // features
    info = jnp.stack([event_node // node_rows, event_node % node_rows, event_bucket])
    info = info.astype(BF).reshape(3 * info_rows, features)
    tail = -(-3 * info_rows // 16) * 16
    packed = jnp.concatenate(
        [edge_features, info, jnp.zeros((tail - 3 * info_rows, features), BF)], axis=0
    )
    arrived = lax.all_gather(packed, "node", axis=0, tiled=False)
    numbers = arrived[:, events : events + 3 * info_rows, :].reshape(devices, 3, events)
    meta = jnp.concatenate(
        [
            numbers[:, 1:, :],
            jnp.ones((devices, 1, events), BF),
            jnp.zeros((devices, 5, events), BF),
        ],
        axis=1,
    )
    owners = numbers[:, 0, :].astype(F32)
    chunk = 256
    new_memory, own_table = pl.pallas_call(
        functools.partial(memory_kernel, devices, events, slots, chunk),
        out_shape=(
            jax.ShapeDtypeStruct((node_rows, columns), BF),
            jax.ShapeDtypeStruct((node_rows * stride, LANES), BF),
        ),
        in_specs=[vmem] * 9,
        out_specs=(vmem, vmem),
        scratch_shapes=[
            pltpu.VMEM((devices, events), F32),
            pltpu.VMEM((devices * slots, features), BF),
            pltpu.VMEM((devices * slots, 8), F32),
            pltpu.VMEM((node_rows, columns), F32),
            pltpu.VMEM((node_rows, LANES), F32),
            pltpu.VMEM((node_rows * stride, LANES), F32),
        ],
        compiler_params=pltpu.CompilerParams(vmem_limit_bytes=VMEM_LIMIT),
        name="memory_step",
    )(
        arrived,
        meta,
        owners,
        node_memory,
        edge_weight,
        time_message,
        input_weight,
        hidden_weight,
        gate_bias.reshape(1, -1),
    )
    whole = lax.all_gather(own_table, "node", axis=0, tiled=True)

    ids = jnp.concatenate([neighbours.T.reshape(-1), event_node]) * stride
    gap = jnp.zeros((events, GROUP - fanout), F32)
    rest = jnp.zeros((events, LANES - HEADS * GROUP), F32)
    logits = jnp.concatenate([affinity, gap] * HEADS + [rest], axis=1)
    buckets = jnp.pad(neighbour_bucket, ((0, 0), (0, LANES - fanout)))
    resident = whole.size * 4 <= RESIDENT_LIMIT
    near_rows = (fanout + 1) * events * stride
    if resident:
        source = whole
        source_spec = pl.BlockSpec(memory_space=pl.ANY)
        extra = [
            pltpu.VMEM(whole.shape, BF),
            pltpu.VMEM(whole.shape, F32),
            pltpu.VMEM((near_rows, LANES), F32),
            pltpu.SemaphoreType.DMA((8,)),
        ]
    else:
        source = whole.reshape(-1, stride, LANES)[ids // stride]
        source = source.reshape(near_rows, LANES).astype(F32)
        source_spec = vmem
        extra = []
    embedding, grads = pl.pallas_call(
        functools.partial(event_kernel, resident, events, fanout),
        out_shape=(
            jax.ShapeDtypeStruct((events, columns), BF),
            jax.ShapeDtypeStruct((4 * columns, columns), BF),
        ),
        in_specs=[smem, source_spec] + [vmem] * 8,
        out_specs=(vmem, vmem),
        scratch_shapes=extra
        + [
            pltpu.VMEM((events, columns), BF),
            pltpu.VMEM((events, columns), BF),
            pltpu.VMEM((events, columns), BF),
            pltpu.VMEM((2 * HEADS, events, columns), F32),
            pltpu.VMEM((2 * HEADS, events, columns), BF),
            pltpu.VMEM((HEADS, events, LANES), BF),
            pltpu.VMEM((HEADS, events, LANES), F32),
        ],
        compiler_params=pltpu.CompilerParams(vmem_limit_bytes=VMEM_LIMIT),
        name="event_step",
    )(
        ids,
        source,
        buckets,
        logits,
        upstream,
        time_key,
        query_weight,
        key_weight,
        value_weight,
        out_weight,
    )
    share = 4 * columns // devices
    factor = 1.0 / math.sqrt(events * devices)
    moved = lax.all_to_all(
        grads.reshape(devices, share, columns), "node", split_axis=0, concat_axis=0, tiled=True
    )
    summed = (jnp.sum(moved.astype(F32), axis=0) * factor).astype(BF)
    total = lax.all_gather(summed, "node", axis=0, tiled=True).astype(F32)
    return (embedding, new_memory) + tuple(
        total[part * columns : (part + 1) * columns] for part in range(4)
    )


def solution(mesh):
    placed = (
        P("node"),
        P("node", None),
        P("node"),
        P("node", None),
        P("node", None),
        P("node", None),
        P("node", None),
        P("node", None),
        P(),
        P(),
        P(),
        P(),
        P(),
        P(),
        P(),
        P(),
        P(),
        P(),
    )
    return jax.shard_map(
        shards,
        mesh=mesh,
        in_specs=placed,
        out_specs=(P("node", None), P("node", None), P(), P(), P(), P()),
        check_vma=False,
    )
```

time: 499 us -> 328 us (0.66)
  the two profiles are of different devices: /device:TPU:0 before, /device:TPU:29 now
where the time goes in v1:
time: 328 us; the launch traced here: 325 us
  waiting for transfers between devices  191 us (58%)
  Pallas kernels  54.8 us (17%)
  blocking collectives  51.2 us (16%)
  between operations  13.9 us (4%)
  local copies, waits for them, and re-layouts  8.51 us (3%)
  other arithmetic  6.1 us (2%)
    all_gather x1, waiting for transfers between devices, shards(): whole = lax.all_gather(own_table, 'node', axis=0, tiled=True)  73 us
    all_gather x1, waiting for transfers between devices, shards(): arrived = lax.all_gather(packed, 'node', axis=0, tiled=False)  61.4 us
    all_gather x1, waiting for transfers between devices, shards(): total = lax.all_gather(summed, 'node', axis=0, tiled=True).astype(F32)  56.3 us
    all_to_all x1, blocking collectives, shards(): lax.all_to_all(grads.reshape(devices, share, columns), 'node', split_axis...  51.2 us
    pallas_call x1, Pallas kernels, shards(): pl.pallas_call(functools.partial(event_kernel, resident, events, fanout),...  43 us
    pallas_call x1, Pallas kernels, shards(): pl.pallas_call(functools.partial(memory_kernel, devices, events, slots, c...  11.8 us
  transfers between devices with their start and end apart: 3, of which 3 were waited for; matrix products, arithmetic and copies ran while one was open for 1% of the time, Pallas kernels for 0%

profile of v1, /device:TPU:29, one launch (start us, length us, event | category | flops | bytes accessed | tf_op | source)
XLA Modules:
  0.0 325.4 jit_solution(6461660317246247327)
XLA Ops:
  7.2 0.0 all-gather.9.cloned.1.call-start
  7.2 0.7 convert.15
  7.9 0.7 fusion.1
  8.7 0.1 pad.10.clone
  8.7 1.7 maximum_maximum_fusion.1
  10.4 0.0 all-gather.9.cloned.1.call-update
  10.5 0.0 all-gather.5.cloned.1.call-start
  10.5 0.1 pad.7.clone
  10.6 0.1 pad.6.clone
  10.7 1.3 reshape.31.gate_bias
  12.0 61.4 %all-gather.9.cloned.1.call-done = bf16[16896,128]{1,0:T(8,128)(2,1)} async-done(((bf16[528,128]{1,0:T(8,128)(2,1)}), bf16[16896,128]{1,0:T(8,128)(2,1)}) %all-gather.9.cloned.1.call-update) | async-done | bytes 4325392 | tf_op jit(solution)/shard_map/all_gather | solution.py:330
  73.4 0.9 slice.28
  74.3 0.1 reshape.30
  74.4 0.1 slice.29
  74.5 0.6 fusion.owners
  75.1 0.8 maximum_maximum_fusion.meta
  75.9 0.0 copy-start.2
  75.9 0.0 copy-start
  75.9 0.0 copy-start.1
  75.9 11.8 %memory_step.1 = (bf16[256,512]{1,0:T(8,128)(2,1)}, bf16[1024,128]{1,0:T(8,128)(2,1)}) custom-call(bf16[32,528,128]{2,1,0:T(8,128)(2,1)} %bitcast.10, bf16[32,8,512]{2,1,0:T(8,128)(2,1)} %maximum_maximum_fusion.meta, f32[32,512]{1,0:T(8,128)} %fusion.owners, bf16[256,512]{1,0:T(8,128)(2,1)} %memory.1, bf16[128,512]{1,0:T(8,128)(2,1)} %edge_weight.1, ...), custom_call_target="tpu_custom_call" | custom-call | tf_op jit(solution)/shard_map/memory_step/pallas_call | solution.py:342
  87.7 0.0 copy-start.3
  87.7 0.0 all-gather.5.cloned.1.call-update
  87.8 0.0 all-gather.7.cloned.1.call-start
  87.8 0.0 copy-done.2
  87.8 0.0 copy-done
  87.8 0.1 copy.29
  88.0 0.0 copy-done.1
  88.0 0.1 copy.30
  88.1 0.7 pad.4.buckets
  88.9 1.0 concatenate.15.affinity
  90.0 0.0 copy-done.3
  90.0 0.6 add_multiply_fusion.ids
  90.6 73.0 %all-gather.5.cloned.1.call-done.source = bf16[32768,128]{1,0:T(8,128)(2,1)} async-done(((bf16[1024,128]{1,0:T(8,128)(2,1)}), bf16[32768,128]{1,0:T(8,128)(2,1)}) %all-gather.5.cloned.1.call-update) | async-done | bytes 8388624 | tf_op jit(solution)/shard_map/all_gather | solution.py:371
  163.6 43.0 %event_step.1 = (bf16[512,512]{1,0:T(8,128)(2,1)}, bf16[2048,512]{1,0:T(8,128)(2,1)}) custom-call(s32[5632]{0:T(1024)} %add_multiply_fusion.ids, bf16[32768,128]{1,0:T(8,128)(2,1)} %all-gather.5.cloned.1.call-done.source, s32[512,128]{1,0:T(8,128)} %pad.4.buckets, f32[512,128]{1,0:T(8,128)} %concatenate.15.affinity, bf16[512,512]{1,0:T(8,128)(2,1)} %upstream.1, ...), custom_call_target="tpu_custom_call" | custom-call | tf_op jit(solution)/shard_map/event_step/pallas_call | solution.py:394
  206.6 51.2 %all_to_all.5 = bf16[32,64,512]{2,1,0:T(8,128)(2,1)S(1)} all-to-all(bf16[32,64,512]{2,1,0:T(8,128)(2,1)} %bitcast.11), channel_id=1, replica_groups=mesh['node'=32] {'node'}, dimensions={0} | all-to-all | bytes 4194304 | tf_op jit(solution)/shard_map/all_to_all | solution.py:428
  257.9 0.3 convert_reduce_fusion
  258.2 0.6 multiply_convert_fusion
  258.8 0.0 all-gather.7.cloned.1.call-update
  258.8 56.3 %all-gather.7.cloned.1.call-done = bf16[2048,512]{1,0:T(8,128)(2,1)} async-done(((bf16[64,512]{1,0:T(8,128)(2,1)}), bf16[2048,512]{1,0:T(8,128)(2,1)}) %all-gather.7.cloned.1.call-update) | async-done | bytes 2097168 | tf_op jit(solution)/shard_map/all_gather | solution.py:432
  315.1 3.7 %fusion.4 = (f32[512,512]{1,0:T(8,128)}, f32[512,512]{1,0:T(8,128)}, f32[512,512]{1,0:T(8,128)}, f32[512,512]{1,0:T(8,128)}) fusion(bf16[2048,512]{1,0:T(8,128)(2,1)} %all-gather.7.cloned.1.call-done), kind=kLoop, calls=%fused_computation.18 | loop fusion | bytes 8388608 | tf_op jit(solution)/shard_map/slice | solution.py:434
  (11 shorter events, 0.1 us)
Async XLA Ops:
  7.2 66.2 %all-gather.9.cloned.1.call-start = ((), (), s32[]{:S(2)}) async-start(), calls=%async_computation.3 | async-start | bytes 4460544 | tf_op jit(solution)/shard_map/all_gather | solution.py:330
  10.5 153.1 %all-gather.5.cloned.1.call-start = ((), (), s32[]{:S(2)}) async-start(), calls=%async_computation.1 | async-start | bytes 8650752 | tf_op jit(solution)/shard_map/all_gather | solution.py:371
  75.9 11.9 %copy-start.2 = (s32[512,10]{0,1:T(8,128)S(1)}, s32[512,10]{0,1:T(8,128)}, u32[]{:S(2)}) copy-start(s32[512,10]{0,1:T(8,128)} %param.19) | copy-start | bytes 61444
  75.9 11.9 %copy-start = (s32[512,10]{0,1:T(8,128)S(1)}, s32[512,10]{0,1:T(8,128)}, u32[]{:S(2)}) copy-start(s32[512,10]{0,1:T(8,128)} %param.21) | copy-start | bytes 61444
  75.9 12.1 %copy-start.1 = (f32[512,10]{0,1:T(8,128)S(1)}, f32[512,10]{0,1:T(8,128)}, u32[]{:S(2)}) copy-start(f32[512,10]{0,1:T(8,128)} %param.23) | copy-start | bytes 61444
  87.7 2.2 copy-start.3
  87.8 227.4 %all-gather.7.cloned.1.call-start = ((), (), s32[]{:S(2)}) async-start(), calls=%async_computation.2 | async-start | bytes 2162688 | tf_op jit(solution)/shard_map/all_gather | solution.py:432
Sparse Core Ops, SparseCore 0:
  11.4 61.8 all-gather.8
  87.9 75.6 all-gather.4
  258.9 56.1 all-gather.6

commit v2 on v1

--- a/solution.py
+++ b/solution.py
@@ -37,14 +37,239 @@
     return high, low
 
 
+def pack_kernel(devices, slots, feats, meta, owners, outgoing, sel):
+    events = feats.shape[0]
+    ids = lax.broadcasted_iota(jnp.int32, (devices, events), 0)
+    theirs = ids == owners[...]
+    before = lax.broadcasted_iota(jnp.int32, (events, events), 0) < lax.broadcasted_iota(
+        jnp.int32, (events, events), 1
+    )
+    rank = mm(theirs.astype(F32).astype(BF), before.astype(F32).astype(BF))
+    sel[...] = jnp.where(theirs, rank, -1.0)
+    slot_ids = lax.broadcasted_iota(jnp.int32, (slots, events), 0).astype(F32)
+    lane_ids = lax.broadcasted_iota(jnp.int32, (LANES, events), 0).astype(F32)
+
+    def pick(step, carry):
+        for part in range(4):
+            device = step * 4 + part
+            row = sel[pl.ds(device, 1), :]
+            hits = (slot_ids == row).astype(F32).astype(BF)
+            outgoing[device, :slots, :] = mm(hits, feats[...]).astype(BF)
+            turned = (lane_ids == row).astype(F32).astype(BF)
+            outgoing[device, slots:, :] = mm_nt(meta[...], turned).astype(BF)
+        return carry
+
+    lax.fori_loop(0, devices // 4, pick, 0)
+
+
+def exchange_kernel(devices, outgoing, inbox, send_sems, recv_sems, own_sem):
+    me = lax.axis_index("node")
+    barrier = pltpu.get_barrier_semaphore()
+
+    def greet(step, carry):
+        pl.semaphore_signal(
+            barrier,
+            inc=1,
+            device_id=(lax.rem(me + step, devices),),
+            device_id_type=pl.DeviceIdType.MESH,
+        )
+        return carry
+
+    lax.fori_loop(1, devices, greet, 0)
+    pl.semaphore_wait(barrier, devices - 1)
+
+    def send(step):
+        peer = lax.rem(me + step, devices)
+        return pltpu.make_async_remote_copy(
+            src_ref=outgoing.at[peer],
+            dst_ref=inbox.at[me],
+            send_sem=send_sems.at[peer],
+            recv_sem=recv_sems.at[me],
+            device_id=(peer,),
+            device_id_type=pl.DeviceIdType.MESH,
+        )
+
+    def receive(step):
+        peer = lax.rem(me + step, devices)
+        return pltpu.make_async_remote_copy(
+            src_ref=outgoing.at[peer],
+            dst_ref=inbox.at[peer],
+            send_sem=send_sems.at[peer],
+            recv_sem=recv_sems.at[peer],
+            device_id=(peer,),
+            device_id_type=pl.DeviceIdType.MESH,
+        )
+
+    def start(step, carry):
+        send(step).start()
+        return carry
+
+    def finish(step, carry):
+        receive(step).wait_recv()
+        send(step).wait_send()
+        return carry
+
+    lax.fori_loop(1, devices, start, 0)
+    own = pltpu.make_async_copy(outgoing.at[me], inbox.at[me], own_sem)
+    own.start()
+    own.wait()
+    lax.fori_loop(1, devices, finish, 0)
+
+
+def reduce_kernel(
+    chips,
+    groups,
+    factor,
+    grads,
+    result,
+    near,
+    pair,
+    landed,
+    share,
+    pair_send,
+    pair_recv,
+    far_send,
+    far_recv,
+    back_send,
+    back_recv,
+    hop_send,
+    hop_recv,
+):
+    me = lax.axis_index("node")
+    core = lax.rem(me, 2)
+    chip = me // 2
+    partner = me + 1 - 2 * core
+    half = grads.shape[0] // 2
+    rows = half // chips
+    group_rows = half // groups
+    mesh_id = pl.DeviceIdType.MESH
+    barrier = pltpu.get_barrier_semaphore()
+
+    def peer_chip(step):
+        return lax.rem(chip + step, chips)
+
+    def greet(step, carry):
+        pl.semaphore_signal(
+            barrier, inc=1, device_id=(2 * peer_chip(step) + core,), device_id_type=mesh_id
+        )
+        return carry
+
+    pl.semaphore_signal(barrier, inc=1, device_id=(partner,), device_id_type=mesh_id)
+    lax.fori_loop(1, chips, greet, 0)
+    pl.semaphore_wait(barrier, chips)
+
+    def half_at(which, first, size):
+        return pl.ds(pl.multiple_of(which * half + first, 16), size)
+
+    def piece(which):
+        return pl.ds(pl.multiple_of(which * rows, 16), rows)
+
+    def swap(group):
+        return pltpu.make_async_remote_copy(
+            src_ref=grads.at[half_at(1 - core, group * group_rows, group_rows)],
+            dst_ref=near.at[pl.ds(group * group_rows, group_rows)],
+            send_sem=pair_send.at[group],
+            recv_sem=pair_recv.at[group],
+            device_id=(partner,),
+            device_id_type=mesh_id,
+        )
+
+    def scatter(target, source):
+        return pltpu.make_async_remote_copy(
+            src_ref=pair.at[piece(target)],
+            dst_ref=landed.at[source],
+            send_sem=far_send.at[target],
+            recv_sem=far_recv.at[source],
+            device_id=(2 * target + core,),
+            device_id_type=mesh_id,
+        )
+
+    def spread(target, source):
+        return pltpu.make_async_remote_copy(
+            src_ref=share,
+            dst_ref=result.at[half_at(core, source * rows, rows)],
+            send_sem=back_send.at[target],
+            recv_sem=back_recv.at[source],
+            device_id=(2 * target + core,),
+            device_id_type=mesh_id,
+        )
+
+    def hop(source, which):
+        return pltpu.make_async_remote_copy(
+            src_ref=result.at[half_at(core, source * rows, rows)],
+            dst_ref=result.at[half_at(which, source * rows, rows)],
+            send_sem=hop_send.at[source],
+            recv_sem=hop_recv.at[source],
+            device_id=(partner,),
+            device_id_type=mesh_id,
+        )
+
+    for group in range(groups):
+        swap(group).start()
+    per_group = chips // groups
+    for group in range(groups):
+        swap(group).wait_recv()
+        at = pl.ds(group * group_rows, group_rows)
+        own = grads[half_at(core, group * group_rows, group_rows), :]
+        pair[at, :] = (own.astype(F32) + near[at, :].astype(F32)).astype(BF)
+        for place in range(per_group):
+            target = group * per_group + place
+
+            @pl.when(target != chip)
+            def _(target=target):
+                scatter(target, chip).start()
+
+    for group in range(groups):
+        swap(group).wait_send()
+    landed[chip] = pair[piece(chip), :]
+
+    def arrive(step, carry):
+        scatter(peer_chip(step), peer_chip(step)).wait_recv()
+        scatter(peer_chip(step), chip).wait_send()
+        return carry
+
+    lax.fori_loop(1, chips, arrive, 0)
+    total = landed[0].astype(F32)
+    for source in range(1, chips):
+        total += landed[source].astype(F32)
+    final = (total * factor).astype(BF)
+    share[...] = final
+    result[half_at(core, chip * rows, rows), :] = final
+
+    def send_share(step, carry):
+        spread(peer_chip(step), chip).start()
+        return carry
+
+    lax.fori_loop(1, chips, send_share, 0)
+    hop(chip, core).start()
+
+    def forward(step, carry):
+        source = lax.rem(chip + chips - step, chips)
+        spread(source, source).wait_recv()
+        hop(source, core).start()
+        return carry
+
+    lax.fori_loop(1, chips, forward, 0)
+
+    def drain(step, carry):
+        hop(step, 1 - core).wait_recv()
+        hop(step, core).wait_send()
+        return carry
+
+    lax.fori_loop(0, chips, drain, 0)
+
+    def drain_share(step, carry):
+        spread(peer_chip(step), chip).wait_send()
+        return carry
+
+    lax.fori_loop(1, chips, drain_share, 0)
+
+
 def memory_kernel(
     devices,
-    events,
     slots,
     chunk,
-    feats,
-    meta,
-    owners,
+    inbox,
     memory,
     edge_weight,
     time_message,
@@ -53,32 +278,26 @@
     gate_bias,
     out_memory,
     out_table,
-    sel,
     picked,
     picked_meta,
     totals,
     counts,
     wide,
 ):
-    me = lax.axis_index("node")
     rows = memory.shape[0]
     columns = memory.shape[1]
     stride = columns // LANES
-    mine = owners[...] == me.astype(F32)
-    before = lax.broadcasted_iota(jnp.int32, (events, events), 0) < lax.broadcasted_iota(
-        jnp.int32, (events, events), 1
-    )
-    rank = mm(mine.astype(F32).astype(BF), before.astype(F32).astype(BF))
-    sel[...] = jnp.where(mine, rank, -1.0)
-    slot_ids = lax.broadcasted_iota(jnp.int32, (slots, events), 0).astype(F32)
+    turn = (
+        lax.broadcasted_iota(jnp.int32, (slots, LANES), 0)
+        == lax.broadcasted_iota(jnp.int32, (slots, LANES), 1)
+    ).astype(F32).astype(BF)
 
     def pick(step, carry):
-        for half in range(4):
-            source = step * 4 + half
-            hits = (slot_ids == sel[pl.ds(source, 1), :]).astype(F32).astype(BF)
+        for part in range(4):
+            source = step * 4 + part
             at = pl.ds(pl.multiple_of(source * slots, slots), slots)
-            picked[at, :] = mm(hits, feats[source, :events, :]).astype(BF)
-            picked_meta[at, :] = mm_nt(hits, meta[source])
+            picked[at, :] = inbox[source, :slots, :]
+            picked_meta[at, :] = mm_nt(turn, inbox[source, slots:, :])
         return carry
 
     lax.fori_loop(0, devices // 4, pick, 0)
@@ -320,37 +539,43 @@
     vmem = pl.BlockSpec(memory_space=pltpu.VMEM)
     smem = pl.BlockSpec(memory_space=pltpu.SMEM)
 
-    info_rows = events // features
-    info = jnp.stack([event_node // node_rows, event_node % node_rows, event_bucket])
-    info = info.astype(BF).reshape(3 * info_rows, features)
-    tail = -(-3 * info_rows // 16) * 16
-    packed = jnp.concatenate(
-        [edge_features, info, jnp.zeros((tail - 3 * info_rows, features), BF)], axis=0
-    )
-    arrived = lax.all_gather(packed, "node", axis=0, tiled=False)
-    numbers = arrived[:, events : events + 3 * info_rows, :].reshape(devices, 3, events)
-    meta = jnp.concatenate(
-        [
-            numbers[:, 1:, :],
-            jnp.ones((devices, 1, events), BF),
-            jnp.zeros((devices, 5, events), BF),
+    info = jnp.stack([event_node % node_rows, event_bucket, jnp.ones_like(event_node)])
+    info = jnp.pad(info.astype(BF), ((0, 13), (0, 0)))
+    owners = (event_node // node_rows).reshape(1, events)
+    message_shape = jax.ShapeDtypeStruct((devices, slots + 16, features), BF)
+    outgoing = pl.pallas_call(
+        functools.partial(pack_kernel, devices, slots),
+        out_shape=message_shape,
+        in_specs=[vmem] * 3,
+        out_specs=vmem,
+        scratch_shapes=[pltpu.VMEM((devices, events), F32)],
+        name="pack_step",
+    )(edge_features, info, owners)
+    inbox = pl.pallas_call(
+        functools.partial(exchange_kernel, devices),
+        out_shape=message_shape,
+        in_specs=[vmem],
+        out_specs=vmem,
+        scratch_shapes=[
+            pltpu.SemaphoreType.DMA((devices,)),
+            pltpu.SemaphoreType.DMA((devices,)),
+            pltpu.SemaphoreType.DMA,
         ],
-        axis=1,
-    )
-    owners = numbers[:, 0, :].astype(F32)
+        compiler_params=pltpu.CompilerParams(collective_id=0, has_side_effects=True),
+        name="exchange_step",
+    )(outgoing)
     chunk = 256
     new_memory, own_table = pl.pallas_call(
-        functools.partial(memory_kernel, devices, events, slots, chunk),
+        functools.partial(memory_kernel, devices, slots, chunk),
         out_shape=(
             jax.ShapeDtypeStruct((node_rows, columns), BF),
             jax.ShapeDtypeStruct((node_rows * stride, LANES), BF),
         ),
-        in_specs=[vmem] * 9,
+        in_specs=[vmem] * 7,
         out_specs=(vmem, vmem),
         scratch_shapes=[
-            pltpu.VMEM((devices, events), F32),
             pltpu.VMEM((devices * slots, features), BF),
-            pltpu.VMEM((devices * slots, 8), F32),
+            pltpu.VMEM((devices * slots, 16), F32),
             pltpu.VMEM((node_rows, columns), F32),
             pltpu.VMEM((node_rows, LANES), F32),
             pltpu.VMEM((node_rows * stride, LANES), F32),
@@ -358,9 +583,7 @@
         compiler_params=pltpu.CompilerParams(vmem_limit_bytes=VMEM_LIMIT),
         name="memory_step",
     )(
-        arrived,
-        meta,
-        owners,
+        inbox,
         node_memory,
         edge_weight,
         time_message,
@@ -423,13 +646,29 @@
         value_weight,
         out_weight,
     )
+    chips = devices // 2
+    groups = 4
     share = 4 * columns // devices
     factor = 1.0 / math.sqrt(events * devices)
-    moved = lax.all_to_all(
-        grads.reshape(devices, share, columns), "node", split_axis=0, concat_axis=0, tiled=True
-    )
-    summed = (jnp.sum(moved.astype(F32), axis=0) * factor).astype(BF)
-    total = lax.all_gather(summed, "node", axis=0, tiled=True).astype(F32)
+    total = pl.pallas_call(
+        functools.partial(reduce_kernel, chips, groups, factor),
+        out_shape=jax.ShapeDtypeStruct((4 * columns, columns), BF),
+        in_specs=[vmem],
+        out_specs=vmem,
+        scratch_shapes=[
+            pltpu.VMEM((2 * columns, columns), BF),
+            pltpu.VMEM((2 * columns, columns), BF),
+            pltpu.VMEM((chips, share, columns), BF),
+            pltpu.VMEM((share, columns), BF),
+            pltpu.SemaphoreType.DMA((groups,)),
+            pltpu.SemaphoreType.DMA((groups,)),
+        ]
+        + [pltpu.SemaphoreType.DMA((chips,)) for _ in range(6)],
+        compiler_params=pltpu.CompilerParams(
+            collective_id=1, has_side_effects=True, vmem_limit_bytes=VMEM_LIMIT
+        ),
+        name="reduce_step",
+    )(grads).astype(F32)
     return (embedding, new_memory) + tuple(
         total[part * columns : (part + 1) * columns] for part in range(4)
     )

time: 328 us -> 238 us (0.73)
  waiting for transfers between devices: 191 us -> 74.4 us
  Pallas kernels: 54.8 us -> 138 us
  blocking collectives: 51.2 us -> 0 us
  other arithmetic: 6.1 us -> 2.64 us
    all_gather x2 -> x0, waiting for transfers between devices: 118 us -> none  [the longest x1 61.4 us: shards(): arrived = lax.all_gather(packed, 'node', axis=0, tiled=False)]
    pallas_call x1 -> x4, Pallas kernels: 11.8 us -> 95.3 us  [the longest x1 61.7 us: shards(): pl.pallas_call(functools.partial(reduce_kernel, chips, groups, factor), o...]
    all_to_all x1 -> x0, blocking collectives: 51.2 us -> none  [shards(): lax.all_to_all(grads.reshape(devices, share, columns), 'node', split_axis...]
  transfers between devices with their start and end apart: 3 -> 1, of which waited for: 3 -> 1; matrix products, arithmetic and copies ran while one was open for 1% -> 1% of each run, Pallas kernels for 0% -> 0%
where the time goes in v2:
time: 238 us; the launch traced here: 237 us
  Pallas kernels  138 us (58%)
  waiting for transfers between devices  74.4 us (31%)
  between operations  14.1 us (6%)
  local copies, waits for them, and re-layouts  7.85 us (3%)
  other arithmetic  2.64 us (1%)
    all_gather x1, waiting for transfers between devices, shards(): whole = lax.all_gather(own_table, 'node', axis=0, tiled=True)  74.3 us
    pallas_call x1, Pallas kernels, shards(): pl.pallas_call(functools.partial(reduce_kernel, chips, groups, factor), o...  61.7 us
    pallas_call x1, Pallas kernels, shards(): pl.pallas_call(functools.partial(event_kernel, resident, events, fanout),...  43.1 us
    pallas_call x1, Pallas kernels, shards(): pl.pallas_call(functools.partial(exchange_kernel, devices), out_shape=mes...  19.4 us
    pallas_call x1, Pallas kernels, shards(): pl.pallas_call(functools.partial(memory_kernel, devices, slots, chunk), o...  9.45 us
  transfers between devices with their start and end apart: 1, of which 1 were waited for; matrix products, arithmetic and copies ran while one was open for 1% of the time, Pallas kernels for 0%

profile of v2, /device:TPU:29, one launch (start us, length us, event | category | flops | bytes accessed | tf_op | source)
XLA Modules:
  0.0 237.4 jit_solution(3420089768601592399)
XLA Ops:
  7.2 0.0 all-gather.2.cloned.1.call-start
  7.2 0.7 convert.11
  7.9 1.3 add_select_fusion
  9.2 1.3 reshape.23.gate_bias
  10.5 0.1 pad.12.clone
  10.5 0.1 maximum_maximum_fusion
  10.6 0.6 pad.8.meta
  11.2 4.7 %pack_step.1.outgoing = bf16[32,64,128]{2,1,0:T(8,128)(2,1)} custom-call(bf16[512,128]{1,0:T(8,128)(2,1)} %feats.1, bf16[16,512]{1,0:T(8,128)(2,1)} %pad.8.meta, s32[1,512]{1,0:T(1,128)} %bitcast.4), custom_call_target="tpu_custom_call" | custom-call | tf_op jit(solution)/shard_map/pack_step/pallas_call | solution.py:546
  15.9 19.4 %exchange_step.1.inbox = bf16[32,64,128]{2,1,0:T(8,128)(2,1)} custom-call(bf16[32,64,128]{2,1,0:T(8,128)(2,1)} %pack_step.1.outgoing), custom_call_target="tpu_custom_call" | custom-call | tf_op jit(solution)/shard_map/exchange_step/pallas_call | solution.py:554
  35.4 0.0 copy-start.2
  35.4 0.0 copy-start
  35.4 0.0 copy-start.1
  35.4 9.4 %memory_step.1 = (bf16[256,512]{1,0:T(8,128)(2,1)}, bf16[1024,128]{1,0:T(8,128)(2,1)}) custom-call(bf16[32,64,128]{2,1,0:T(8,128)(2,1)} %exchange_step.1.inbox, bf16[256,512]{1,0:T(8,128)(2,1)} %memory.1, bf16[128,512]{1,0:T(8,128)(2,1)} %edge_weight.1, f32[128,512]{1,0:T(8,128)} %time_message.1, bf16[512,1536]{1,0:T(8,128)(2,1)} %input_weight.1, ...), custom_call_target="tpu_custom_call" | custom-call | tf_op jit(solution)/shard_map/memory_step/pallas_call | solution.py:568
  44.8 0.0 copy-start.3
  44.8 0.0 all-gather.2.cloned.1.call-update
  44.9 0.0 copy-done.2
  44.9 0.0 copy-done
  44.9 0.1 copy.24
  45.0 0.0 copy-done.1
  45.1 0.1 copy.25
  45.2 0.7 pad.9.buckets
  46.0 1.0 concatenate.7.affinity
  47.0 0.0 copy-done.3
  47.0 0.6 add_multiply_fusion.ids
  47.6 74.3 %all-gather.2.cloned.1.call-done.source = bf16[32768,128]{1,0:T(8,128)(2,1)} async-done(((bf16[1024,128]{1,0:T(8,128)(2,1)}), bf16[32768,128]{1,0:T(8,128)(2,1)}) %all-gather.2.cloned.1.call-update) | async-done | bytes 8388624 | tf_op jit(solution)/shard_map/all_gather | solution.py:594
  122.0 43.1 %event_step.1 = (bf16[512,512]{1,0:T(8,128)(2,1)}, bf16[2048,512]{1,0:T(8,128)(2,1)}) custom-call(s32[5632]{0:T(1024)} %add_multiply_fusion.ids, bf16[32768,128]{1,0:T(8,128)(2,1)} %all-gather.2.cloned.1.call-done.source, s32[512,128]{1,0:T(8,128)} %pad.9.buckets, f32[512,128]{1,0:T(8,128)} %concatenate.7.affinity, bf16[512,512]{1,0:T(8,128)(2,1)} %upstream.1, ...), custom_call_target="tpu_custom_call" | custom-call | tf_op jit(solution)/shard_map/event_step/pallas_call | solution.py:617
  165.0 61.7 %reduce_step.1 = bf16[2048,512]{1,0:T(8,128)(2,1)} custom-call(bf16[2048,512]{1,0:T(8,128)(2,1)} %get-tuple-element.13.grads), custom_call_target="tpu_custom_call" | custom-call | tf_op jit(solution)/shard_map/reduce_step/pallas_call | solution.py:653
  226.8 3.8 %fusion.2 = (f32[512,512]{1,0:T(8,128)}, f32[512,512]{1,0:T(8,128)}, f32[512,512]{1,0:T(8,128)}, f32[512,512]{1,0:T(8,128)}) fusion(bf16[2048,512]{1,0:T(8,128)(2,1)} %reduce_step.1), kind=kLoop, calls=%fused_computation.11 | loop fusion | bytes 8388608 | tf_op jit(solution)/shard_map/slice | solution.py:673
  (5 shorter events, 0.1 us)
Async XLA Ops:
  7.2 114.8 %all-gather.2.cloned.1.call-start = ((), (), s32[]{:S(2)}) async-start(), calls=%async_computation | async-start | bytes 8650752 | tf_op jit(solution)/shard_map/all_gather | solution.py:594
  35.4 9.5 %copy-start.2 = (s32[512,10]{0,1:T(8,128)S(1)}, s32[512,10]{0,1:T(8,128)}, u32[]{:S(2)}) copy-start(s32[512,10]{0,1:T(8,128)} %param.19) | copy-start | bytes 61444
  35.4 9.5 %copy-start = (s32[512,10]{0,1:T(8,128)S(1)}, s32[512,10]{0,1:T(8,128)}, u32[]{:S(2)}) copy-start(s32[512,10]{0,1:T(8,128)} %param.21) | copy-start | bytes 61444
  35.4 9.7 %copy-start.1 = (f32[512,10]{0,1:T(8,128)S(1)}, f32[512,10]{0,1:T(8,128)}, u32[]{:S(2)}) copy-start(f32[512,10]{0,1:T(8,128)} %param.23) | copy-start | bytes 61444
  44.8 2.2 copy-start.3
Sparse Core Ops, SparseCore 0:
  45.0 76.9 all-gather.1

commit v3 on v2

--- a/solution.py
+++ b/solution.py
@@ -345,6 +345,128 @@
     for part in range(stride):
         wide[pl.ds(part, rows, stride=stride), :] = fresh[:, part * LANES : (part + 1) * LANES]
     out_table[...] = wide[...].astype(BF)
+
+
+def gather_kernel(
+    line,
+    side,
+    subs,
+    own,
+    whole,
+    recv,
+    hop_recv,
+    line_send,
+    first_send,
+    second_send,
+    hop_send,
+    own_sem,
+):
+    me = lax.axis_index("node")
+    core = lax.rem(me, 2)
+    chip = me // 2
+    partner = me + 1 - 2 * core
+    low, mid, far = lax.rem(chip, side), lax.rem(chip // side, side), chip // (side * side)
+    first = (1 - core) * low + core * mid
+    second = (1 - core) * mid + core * low
+    first_stride = 1 + core * (side - 1)
+    second_stride = side - core * (side - 1)
+    rows = own.shape[0]
+    size = rows // subs
+    mesh_id = pl.DeviceIdType.MESH
+
+    def chip_of(along, over, across):
+        return (
+            lax.rem(far + line - along, line) * side * side
+            + lax.rem(first + side - over, side) * first_stride
+            + lax.rem(second + side - across, side) * second_stride
+        )
+
+    peers = [2 * chip_of(line - step, 0, 0) + core for step in range(1, line)]
+    first_peers = [2 * chip_of(0, side - step, 0) + core for step in range(1, side)]
+    second_peers = [2 * chip_of(0, 0, side - step) + core for step in range(1, side)]
+    everyone = peers + first_peers + second_peers + [partner]
+    barrier = pltpu.get_barrier_semaphore()
+    for device in everyone:
+        pl.semaphore_signal(barrier, inc=1, device_id=(device,), device_id_type=mesh_id)
+    pl.semaphore_wait(barrier, len(everyone))
+
+    def at(source, part, kind):
+        return pl.ds(pl.multiple_of((2 * source + kind) * rows + part * size, 16), size)
+
+    def copy(source, part, mine, send_sem, device):
+        src = own.at[pl.ds(part * size, size)] if mine else whole.at[at(source, part, core)]
+        return pltpu.make_async_remote_copy(
+            src_ref=src,
+            dst_ref=whole.at[at(source, part, core)],
+            send_sem=send_sem,
+            recv_sem=recv.at[source * subs + part],
+            device_id=(device,),
+            device_id_type=mesh_id,
+        )
+
+    def hop(source, part, mine, kind):
+        src = own.at[pl.ds(part * size, size)] if mine else whole.at[at(source, part, kind)]
+        return pltpu.make_async_remote_copy(
+            src_ref=src,
+            dst_ref=whole.at[at(source, part, kind)],
+            send_sem=hop_send.at[source * subs + part],
+            recv_sem=hop_recv.at[source * subs + part],
+            device_id=(partner,),
+            device_id_type=mesh_id,
+        )
+
+    started = []
+
+    def start(made):
+        made.start()
+        started.append(made)
+
+    def landed(source, part):
+        copy(source, part, False, hop_send.at[0], partner).wait_recv()
+
+    stay = pltpu.make_async_copy(own, whole.at[pl.ds(pl.multiple_of(me * rows, 16), rows)], own_sem)
+    stay.start()
+    steps = line * subs
+    for step in range(steps + 2):
+        if step < steps:
+            along, part = divmod(step, subs)
+            source = chip_of(along, 0, 0)
+            mine = along == 0
+            if not mine:
+                landed(source, part)
+            for to, device in enumerate(first_peers):
+                start(copy(source, part, mine, first_send.at[step, to], device))
+            if mine:
+                for to, device in enumerate(peers):
+                    start(copy(source, part, mine, line_send.at[part, to], device))
+            for to, device in enumerate(second_peers):
+                start(copy(source, part, mine, second_send.at[step, 0, to], device))
+            start(hop(source, part, mine, core))
+        if 0 <= step - 1 < steps:
+            along, part = divmod(step - 1, subs)
+            for over in range(1, side):
+                source = chip_of(along, over, 0)
+                landed(source, part)
+                for to, device in enumerate(second_peers):
+                    start(copy(source, part, False, second_send.at[step - 1, over, to], device))
+                start(hop(source, part, False, core))
+        if 0 <= step - 2 < steps:
+            along, part = divmod(step - 2, subs)
+            for across in range(1, side):
+                for over in range(side):
+                    source = chip_of(along, over, across)
+                    landed(source, part)
+                    start(hop(source, part, False, core))
+    stay.wait()
+    for made in started:
+        made.wait_send()
+
+    def drain(source, carry):
+        for part in range(subs):
+            hop(source, part, False, 1 - core).wait_recv()
+        return carry
+
+    lax.fori_loop(0, line * side * side, drain, 0)
 
 
 def event_kernel(
@@ -591,7 +713,27 @@
         hidden_weight,
         gate_bias.reshape(1, -1),
     )
-    whole = lax.all_gather(own_table, "node", axis=0, tiled=True)
+    chips = devices // 2
+    side = max(s for s in range(1, chips + 1) if chips % (s * s) == 0 and s**3 <= chips)
+    line = chips // (side * side)
+    subs = 2
+    whole = pl.pallas_call(
+        functools.partial(gather_kernel, line, side, subs),
+        out_shape=jax.ShapeDtypeStruct((devices * node_rows * stride, LANES), BF),
+        in_specs=[vmem],
+        out_specs=pl.BlockSpec(memory_space=pl.ANY),
+        scratch_shapes=[
+            pltpu.SemaphoreType.DMA((chips * subs,)),
+            pltpu.SemaphoreType.DMA((chips * subs,)),
+            pltpu.SemaphoreType.DMA((subs, line - 1)),
+            pltpu.SemaphoreType.DMA((line * subs, side - 1)),
+            pltpu.SemaphoreType.DMA((line * subs, side, side - 1)),
+            pltpu.SemaphoreType.DMA((chips * subs,)),
+            pltpu.SemaphoreType.DMA,
+        ],
+        compiler_params=pltpu.CompilerParams(collective_id=2, has_side_effects=True),
+        name="gather_step",
+    )(own_table)
 
     ids = jnp.concatenate([neighbours.T.reshape(-1), event_node]) * stride
     gap = jnp.zeros((events, GROUP - fanout), F32)
@@ -646,7 +788,6 @@
         value_weight,
         out_weight,
     )
-    chips = devices // 2
     groups = 4
     share = 4 * columns // devices
     factor = 1.0 / math.sqrt(events * devices)

time: 238 us -> 203 us (0.85)
  waiting for transfers between devices: 74.4 us -> 0 us
  Pallas kernels: 138 us -> 189 us
  between operations: 14.1 us -> 0.7 us
    all_gather x1 -> x0, waiting for transfers between devices: 74.3 us -> none  [shards(): whole = lax.all_gather(own_table, 'node', axis=0, tiled=True)]
    pallas_call x0 -> x1, Pallas kernels: none -> 47.6 us  [shards(): pl.pallas_call(functools.partial(gather_kernel, line, side, subs), out_sh...]
    pallas_call x1, Pallas kernels: 61.7 us -> 64.4 us  [shards(): pl.pallas_call(functools.partial(reduce_kernel, chips, groups, factor), o...]
  transfers between devices with their start and end apart: 1 -> 0, of which waited for: 1 -> 0; matrix products, arithmetic and copies ran while one was open for 1% -> 0% of each run, Pallas kernels for 0% -> 0%
where the time goes in v3:
time: 203 us
  Pallas kernels  189 us (93%)
  local copies, waits for them, and re-layouts  10.1 us (5%)
  other arithmetic  3.31 us (2%)
    pallas_call x1, Pallas kernels, shards(): pl.pallas_call(functools.partial(reduce_kernel, chips, groups, factor), o...  64.4 us
    pallas_call x1, Pallas kernels, shards(): pl.pallas_call(functools.partial(gather_kernel, line, side, subs), out_sh...  47.6 us
    pallas_call x1, Pallas kernels, shards(): pl.pallas_call(functools.partial(event_kernel, resident, events, fanout),...  43.1 us
    pallas_call x1, Pallas kernels, shards(): pl.pallas_call(functools.partial(exchange_kernel, devices), out_shape=mes...  19.4 us
    pallas_call x1, Pallas kernels, shards(): pl.pallas_call(functools.partial(memory_kernel, devices, slots, chunk), o...  9.44 us
    pallas_call x1, Pallas kernels, shards(): pl.pallas_call(functools.partial(pack_kernel, devices, slots), out_shape=...  4.71 us

profile of v3, /device:TPU:29, one launch (start us, length us, event | category | flops | bytes accessed | tf_op | source)
XLA Modules:
  0.0 202.8 jit_solution(10230311489782240109)
XLA Ops:
  0.6 0.1 pad.12.clone
  0.7 0.7 convert.11
  1.4 1.3 add_select_fusion
  2.7 0.1 maximum_maximum_fusion
  2.7 1.3 reshape.23.gate_bias
  4.0 0.6 pad.8.meta
  4.6 0.8 reshape.21
  5.4 1.3 add_multiply_fusion.ids
  6.7 0.9 copy.24
  7.6 0.7 pad.9.buckets
  8.3 0.9 copy.25
  9.3 1.0 concatenate.7.affinity
  10.3 4.7 %pack_step.1.outgoing = bf16[32,64,128]{2,1,0:T(8,128)(2,1)} custom-call(bf16[512,128]{1,0:T(8,128)(2,1)} %feats.1, bf16[16,512]{1,0:T(8,128)(2,1)} %pad.8.meta, s32[1,512]{1,0:T(1,128)} %bitcast.4), custom_call_target="tpu_custom_call" | custom-call | tf_op jit(solution)/shard_map/pack_step/pallas_call | solution.py:668
  15.0 19.4 %exchange_step.1.inbox = bf16[32,64,128]{2,1,0:T(8,128)(2,1)} custom-call(bf16[32,64,128]{2,1,0:T(8,128)(2,1)} %pack_step.1.outgoing), custom_call_target="tpu_custom_call" | custom-call | tf_op jit(solution)/shard_map/exchange_step/pallas_call | solution.py:676
  34.4 9.4 %memory_step.1 = (bf16[256,512]{1,0:T(8,128)(2,1)}, bf16[1024,128]{1,0:T(8,128)(2,1)}) custom-call(bf16[32,64,128]{2,1,0:T(8,128)(2,1)} %exchange_step.1.inbox, bf16[256,512]{1,0:T(8,128)(2,1)} %memory.1, bf16[128,512]{1,0:T(8,128)(2,1)} %edge_weight.1, f32[128,512]{1,0:T(8,128)} %time_message.1, bf16[512,1536]{1,0:T(8,128)(2,1)} %input_weight.1, ...), custom_call_target="tpu_custom_call" | custom-call | tf_op jit(solution)/shard_map/memory_step/pallas_call | solution.py:690
  43.9 47.6 %gather_step.1.source = bf16[32768,128]{1,0:T(8,128)(2,1)} custom-call(bf16[1024,128]{1,0:T(8,128)(2,1)} %get-tuple-element.10.own), custom_call_target="tpu_custom_call" | custom-call | tf_op jit(solution)/shard_map/gather_step/pallas_call | solution.py:720
  91.5 43.1 %event_step.1 = (bf16[512,512]{1,0:T(8,128)(2,1)}, bf16[2048,512]{1,0:T(8,128)(2,1)}) custom-call(s32[5632]{0:T(1024)} %add_multiply_fusion.ids, bf16[32768,128]{1,0:T(8,128)(2,1)} %gather_step.1.source, s32[512,128]{1,0:T(8,128)} %pad.9.buckets, f32[512,128]{1,0:T(8,128)} %concatenate.7.affinity, bf16[512,512]{1,0:T(8,128)(2,1)} %upstream.1, ...), custom_call_target="tpu_custom_call" | custom-call | tf_op jit(solution)/shard_map/event_step/pallas_call | solution.py:759
  134.6 64.4 %reduce_step.1 = bf16[2048,512]{1,0:T(8,128)(2,1)} custom-call(bf16[2048,512]{1,0:T(8,128)(2,1)} %get-tuple-element.13.grads), custom_call_target="tpu_custom_call" | custom-call | tf_op jit(solution)/shard_map/reduce_step/pallas_call | solution.py:794
  199.0 3.8 %fusion.2 = (f32[512,512]{1,0:T(8,128)}, f32[512,512]{1,0:T(8,128)}, f32[512,512]{1,0:T(8,128)}, f32[512,512]{1,0:T(8,128)}) fusion(bf16[2048,512]{1,0:T(8,128)(2,1)} %reduce_step.1), kind=kLoop, calls=%fused_computation.11 | loop fusion | bytes 8388608 | tf_op jit(solution)/shard_map/slice | solution.py:814
  (4 shorter events, 0.0 us)
